TPU v7x, 128 devices: a whole 4x4x4 slice. The times are simulated.
128 devices in a mesh: row: 8 (over y, core), col: 16 (over z, x).
Axes of the slice: x: 4, y: 4, z: 4, core: 2. Of those that a mesh axis runs over, the one named last changes fastest.
Arguments:
- features: float32 [16384, 512], P('row'), may hold values from -6 to 6
- jitter: float32 [16384], P('row'), may hold values from 0.25 to 2
Outputs:
- lower: float32 [16384, 2048], P('row', 'col')
- ahead: float32 [16384, 2048], P('row', 'col')
All inputs are finite; a program needn't handle non-finite values.
Results may differ from a plain program's by a relative error of at most 0.0003.
Values sent between devices are 32-bit elements; how exact they have to be, the bound alone decides.
No kernel may reach another device: no remote copies, remote signals or barrier semaphores. Data moves between devices by JAX's collectives and lax.ppermute only.
A program may use at most 256 MiB of HBM per device.

v0:
```python
import jax
import jax.numpy as jnp
from jax import lax
from jax.sharding import PartitionSpec as P

PANEL = 2048


def from_root(x, axis, root):
    mine = lax.axis_index(axis) == root
    return lax.psum(jnp.where(mine, x, jnp.zeros_like(x)), axis)


def kernel_block(left_rows, right_rows):
    products = jnp.dot(
        left_rows, right_rows.T, precision=lax.Precision.HIGHEST, preferred_element_type=jnp.float32
    )
    left_square = jnp.sum(left_rows * left_rows, axis=1)
    right_square = jnp.sum(right_rows * right_rows, axis=1)
    distance = left_square[:, None] + right_square[None, :] - 2.0 * products
    return jnp.exp(-distance / left_rows.shape[1])


def local(features, jitter):
    n_rowdev = lax.axis_size("row")
    n_coldev = lax.axis_size("col")
    local_rows = features.shape[0]
    band_rows = PANEL // n_rowdev
    slab_cols = PANEL // n_coldev
    below_count = local_rows - band_rows
    row_id = lax.axis_index("row")
    col_id = lax.axis_index("col")
    panel_feats, panel_jitter = (
        lax.all_gather(features[:band_rows], "row", axis=0, tiled=True),
        lax.all_gather(jitter[:band_rows], "row", axis=0, tiled=True),
    )
    diag_mask = lax.broadcasted_iota(jnp.int32, (PANEL, PANEL), 0) == lax.broadcasted_iota(
        jnp.int32, (PANEL, PANEL), 1
    )
    diag_block = jnp.where(
        diag_mask, 1.0 + panel_jitter[:, None], kernel_block(panel_feats, panel_feats)
    )
    factor = jnp.linalg.cholesky(diag_block)
    below_feats = features[band_rows:]
    owner_row = col_id * slab_cols // band_rows
    offset = col_id * slab_cols % band_rows
    ahead_piece = lax.dynamic_slice_in_dim(features, band_rows + offset, slab_cols, 0)
    ahead_feats = from_root(ahead_piece, "row", owner_row)
    ahead_tile = kernel_block(below_feats, ahead_feats)
    row_pos = lax.broadcasted_iota(jnp.int32, (below_count, slab_cols), 0)
    col_pos = lax.broadcasted_iota(jnp.int32, (below_count, slab_cols), 1)
    match_mask = (row_pos < band_rows) & (
        row_id * band_rows + row_pos == col_id * slab_cols + col_pos
    )
    ahead_tile = jnp.where(match_mask, 1.0 + jitter[band_rows:][:, None], ahead_tile)
    own_cols = lax.dynamic_slice_in_dim(panel_feats, col_id * slab_cols, slab_cols, 0)
    own_tile = kernel_block(below_feats, own_cols)
    factor_rows = lax.dynamic_slice_in_dim(factor, col_id * slab_cols, slab_cols, 0)
    own_diag = lax.dynamic_slice_in_dim(factor_rows, col_id * slab_cols, slab_cols, 1)

    def finish_slab(pending):
        return lax.linalg.triangular_solve(
            own_diag, pending, left_side=False, lower=True, transpose_a=True
        )

    def empty_slab(pending):
        return jnp.zeros_like(pending)

    def chain_step(source, carry):
        pending, collected = carry
        candidate = lax.cond(source == col_id, finish_slab, empty_slab, pending)
        finished = from_root(candidate, "col", source)
        coupling = lax.dynamic_slice_in_dim(factor_rows, source * slab_cols, slab_cols, 1)
        pending = pending - jnp.dot(
            finished,
            coupling.T,
            precision=lax.Precision.HIGHEST,
            preferred_element_type=jnp.float32,
        )
        collected = lax.dynamic_update_slice_in_dim(collected, finished, source * slab_cols, 1)
        return (pending, collected)

    start_carry = (own_tile, jnp.zeros((below_count, PANEL), jnp.float32))
    unused_pending, lower_below = lax.fori_loop(0, n_coldev, chain_step, start_carry)
    own_slab = lax.dynamic_slice_in_dim(lower_below, col_id * slab_cols, slab_cols, 1)
    factor_piece = lax.dynamic_slice_in_dim(lower_below, offset, slab_cols, 0)
    ahead_lower = from_root(factor_piece, "row", owner_row)
    ahead_below = ahead_tile - jnp.dot(
        lower_below,
        ahead_lower.T,
        precision=lax.Precision.HIGHEST,
        preferred_element_type=jnp.float32,
    )
    top_rows = lax.dynamic_slice(
        factor, (row_id * band_rows, col_id * slab_cols), (band_rows, slab_cols)
    )
    lower_out = jnp.concatenate([top_rows, own_slab], axis=0)
    ahead_out = jnp.concatenate(
        [jnp.zeros((band_rows, slab_cols), jnp.float32), ahead_below], axis=0
    )
    return (lower_out, ahead_out)


def solution(mesh):
    return jax.shard_map(
        local,
        mesh=mesh,
        in_specs=(P("row", None), P("row")),
        out_specs=(P("row", "col"), P("row", "col")),
        check_vma=False,
    )
```

profile of v0, /device:TPU:1, one launch (start us, length us, event | category | flops | bytes accessed | tf_op | source)
XLA Modules:
  0.0 2343.1 jit_solution(17172953472676323570)
XLA Ops:
  9.8 12.1 all-gather
  26.7 19.2 all-gather.3.cloned.1.call-done
  48.5 36.2 %broadcast_add_fusion = (f32[2048,2048]{0,1:T(8,128)}, f32[2048,2048]{0,1:T(8,128)}, f32[2048,2048]{1,0:T(8,128)}) fusion(f32[2048]{0:T(1024)S(1)} %multiply_reduce_fusion, f32[2048,512]{1,0:T(8,128)} %all-gather.3.cloned.1.call-done), kind=kOutput, calls=%fused_computation.16 | convolution fusion | flops 25786580992 | bytes 54534144 | tf_op jit(solution)/shard_map/dot_general | solution.py:15
  84.7 17.6 copy.10
  102.3 17.6 copy.11
  119.9 18.7 add_multiply_fusion
  144.3 11.7 cholesky.457
  156.0 9.8 custom-call.126
  165.9 7.8 cholesky.487
  179.0 11.9 cholesky.480
  191.5 9.8 custom-call.127
  206.6 11.7 cholesky.503
  219.7 9.8 custom-call.128
  235.8 11.7 cholesky.524
  248.8 9.8 custom-call.129
  265.6 11.7 cholesky.962
  278.6 9.8 custom-call.130
  295.5 11.9 cholesky.982
  308.7 9.8 custom-call.131
  325.7 11.7 cholesky.1002
  338.7 10.0 custom-call.132
  350.2 6.0 fusion.30
  356.2 11.7 cholesky.1022
  369.2 10.2 custom-call.133
  386.7 11.7 cholesky.1042
  399.7 9.8 custom-call.134
  410.8 6.1 fusion.93
  416.9 11.7 cholesky.1062
  429.9 9.8 custom-call.135
  446.8 11.7 cholesky.1082
  459.8 9.8 custom-call.136
  476.1 12.1 cholesky.1102
  489.4 9.8 custom-call.137
  505.1 11.7 cholesky.1122
  518.1 9.9 custom-call.138
  533.3 11.7 cholesky.1142
  546.3 9.8 custom-call.139
  560.4 11.9 cholesky.1162
  573.6 9.8 custom-call.140
  586.9 11.7 cholesky.1180
  610.4 7.6 select_select_fusion
  628.9 6.2 broadcast_in_dim.40
  635.1 1616.8 %while.15 = (s32[]{:T(128)}, f32[1792,128]{1,0:T(8,128)S(1)}, f32[1792,2048]{0,1:T(8,128)}, s32[]{:T(128)}, f32[128,128]{1,0:T(8,128)S(1)}, /*index=5*/f32[128,2...) while((s32[]{:T(128)}, f32[1792,128]{1,0:T(8,128)S(1)}, ...), condition=%wide.region_39.40_spmd, body=%wide.region_35.39_spmd.sunk | while | flops 705363968 | bytes 14024975 | solution.py:84
  635.1 10.8 conditional.2
  635.1 9.8 custom-call.110
  646.9 79.6 %all-reduce.8.cloned.1.call-done = f32[1792,128]{0,1:T(8,128)} async-done(((f32[1792,128]{0,1:T(8,128)}), f32[1792,128]{0,1:T(8,128)}) %all-reduce.8.cloned.1.call-update) | async-done | bytes 917520 | tf_op jit(solution)/shard_map/while/body/eval_jaxpr/psum | solution.py:11
  732.8 93.9 %all-reduce.8.cloned.1.call-done = f32[1792,128]{0,1:T(8,128)} async-done(((f32[1792,128]{0,1:T(8,128)}), f32[1792,128]{0,1:T(8,128)}) %all-reduce.8.cloned.1.call-update) | async-done | bytes 917520 | tf_op jit(solution)/shard_map/while/body/eval_jaxpr/psum | solution.py:11
  833.1 94.8 %all-reduce.8.cloned.1.call-done = f32[1792,128]{0,1:T(8,128)} async-done(((f32[1792,128]{0,1:T(8,128)}), f32[1792,128]{0,1:T(8,128)}) %all-reduce.8.cloned.1.call-update) | async-done | bytes 917520 | tf_op jit(solution)/shard_map/while/body/eval_jaxpr/psum | solution.py:11
  934.2 95.2 %all-reduce.8.cloned.1.call-done = f32[1792,128]{0,1:T(8,128)} async-done(((f32[1792,128]{0,1:T(8,128)}), f32[1792,128]{0,1:T(8,128)}) %all-reduce.8.cloned.1.call-update) | async-done | bytes 917520 | tf_op jit(solution)/shard_map/while/body/eval_jaxpr/psum | solution.py:11
  1035.7 93.9 %all-reduce.8.cloned.1.call-done = f32[1792,128]{0,1:T(8,128)} async-done(((f32[1792,128]{0,1:T(8,128)}), f32[1792,128]{0,1:T(8,128)}) %all-reduce.8.cloned.1.call-update) | async-done | bytes 917520 | tf_op jit(solution)/shard_map/while/body/eval_jaxpr/psum | solution.py:11
  1135.9 93.7 %all-reduce.8.cloned.1.call-done = f32[1792,128]{0,1:T(8,128)} async-done(((f32[1792,128]{0,1:T(8,128)}), f32[1792,128]{0,1:T(8,128)}) %all-reduce.8.cloned.1.call-update) | async-done | bytes 917520 | tf_op jit(solution)/shard_map/while/body/eval_jaxpr/psum | solution.py:11
  1235.9 94.9 %all-reduce.8.cloned.1.call-done = f32[1792,128]{0,1:T(8,128)} async-done(((f32[1792,128]{0,1:T(8,128)}), f32[1792,128]{0,1:T(8,128)}) %all-reduce.8.cloned.1.call-update) | async-done | bytes 917520 | tf_op jit(solution)/shard_map/while/body/eval_jaxpr/psum | solution.py:11
  1337.2 94.7 %all-reduce.8.cloned.1.call-done = f32[1792,128]{0,1:T(8,128)} async-done(((f32[1792,128]{0,1:T(8,128)}), f32[1792,128]{0,1:T(8,128)}) %all-reduce.8.cloned.1.call-update) | async-done | bytes 917520 | tf_op jit(solution)/shard_map/while/body/eval_jaxpr/psum | solution.py:11
  1438.2 94.6 %all-reduce.8.cloned.1.call-done = f32[1792,128]{0,1:T(8,128)} async-done(((f32[1792,128]{0,1:T(8,128)}), f32[1792,128]{0,1:T(8,128)}) %all-reduce.8.cloned.1.call-update) | async-done | bytes 917520 | tf_op jit(solution)/shard_map/while/body/eval_jaxpr/psum | solution.py:11
  1539.1 95.0 %all-reduce.8.cloned.1.call-done = f32[1792,128]{0,1:T(8,128)} async-done(((f32[1792,128]{0,1:T(8,128)}), f32[1792,128]{0,1:T(8,128)}) %all-reduce.8.cloned.1.call-update) | async-done | bytes 917520 | tf_op jit(solution)/shard_map/while/body/eval_jaxpr/psum | solution.py:11
  1640.5 96.4 %all-reduce.8.cloned.1.call-done = f32[1792,128]{0,1:T(8,128)} async-done(((f32[1792,128]{0,1:T(8,128)}), f32[1792,128]{0,1:T(8,128)}) %all-reduce.8.cloned.1.call-update) | async-done | bytes 917520 | tf_op jit(solution)/shard_map/while/body/eval_jaxpr/psum | solution.py:11
  1743.2 96.4 %all-reduce.8.cloned.1.call-done = f32[1792,128]{0,1:T(8,128)} async-done(((f32[1792,128]{0,1:T(8,128)}), f32[1792,128]{0,1:T(8,128)}) %all-reduce.8.cloned.1.call-update) | async-done | bytes 917520 | tf_op jit(solution)/shard_map/while/body/eval_jaxpr/psum | solution.py:11
  1846.0 95.2 %all-reduce.8.cloned.1.call-done = f32[1792,128]{0,1:T(8,128)} async-done(((f32[1792,128]{0,1:T(8,128)}), f32[1792,128]{0,1:T(8,128)}) %all-reduce.8.cloned.1.call-update) | async-done | bytes 917520 | tf_op jit(solution)/shard_map/while/body/eval_jaxpr/psum | solution.py:11
  1947.5 94.9 %all-reduce.8.cloned.1.call-done = f32[1792,128]{0,1:T(8,128)} async-done(((f32[1792,128]{0,1:T(8,128)}), f32[1792,128]{0,1:T(8,128)}) %all-reduce.8.cloned.1.call-update) | async-done | bytes 917520 | tf_op jit(solution)/shard_map/while/body/eval_jaxpr/psum | solution.py:11
  2048.6 96.0 %all-reduce.8.cloned.1.call-done = f32[1792,128]{0,1:T(8,128)} async-done(((f32[1792,128]{0,1:T(8,128)}), f32[1792,128]{0,1:T(8,128)}) %all-reduce.8.cloned.1.call-update) | async-done | bytes 917520 | tf_op jit(solution)/shard_map/while/body/eval_jaxpr/psum | solution.py:11
  2151.1 95.6 %all-reduce.8.cloned.1.call-done = f32[1792,128]{0,1:T(8,128)} async-done(((f32[1792,128]{0,1:T(8,128)}), f32[1792,128]{0,1:T(8,128)}) %all-reduce.8.cloned.1.call-update) | async-done | bytes 917520 | tf_op jit(solution)/shard_map/while/body/eval_jaxpr/psum | solution.py:11
  2254.2 15.4 copy.13
  2272.0 45.7 %all-reduce.6.cloned.1.call-done = (f32[128,2048]{0,1:T(8,128)}, f32[128,512]{1,0:T(8,128)}) async-done(((f32[128,2048]{0,1:T(8,128)}, f32[128,512]{1,0:T(8,128)}), (f32[128,2048]{0,1:T(8,128)}, f32[128,512]{1,0:T(8,128)})) %all-reduce.6.cloned.1.call-update) | async-done | bytes 1310736 | tf_op jit(solution)/shard_map/psum | solution.py:11
  2317.7 13.0 fusion.159
  (224 shorter events, 239.0 us)
Async XLA Ops:
  7.2 38.8 %all-gather.3.cloned.1.call-start = ((), (), s32[]{:S(2)}) async-start(), calls=%async_computation | async-start | bytes 4718592 | tf_op jit(solution)/shard_map/all_gather | solution.py:34
  138.6 5.7 copy-start
  610.4 13.4 copy-start.1
  618.1 5.7 copy-start.3
  635.1 91.4 %all-reduce.8.cloned.1.call-start = ((), (), s32[]{:S(2)}) async-start(), calls=%async_computation.2 | async-start | bytes 1835008 | tf_op jit(solution)/shard_map/while/body/eval_jaxpr/psum | solution.py:11
  731.7 95.0 %all-reduce.8.cloned.1.call-start = ((), (), s32[]{:S(2)}) async-start(), calls=%async_computation.2 | async-start | bytes 1835008 | tf_op jit(solution)/shard_map/while/body/eval_jaxpr/psum | solution.py:11
  832.0 95.9 %all-reduce.8.cloned.1.call-start = ((), (), s32[]{:S(2)}) async-start(), calls=%async_computation.2 | async-start | bytes 1835008 | tf_op jit(solution)/shard_map/while/body/eval_jaxpr/psum | solution.py:11
  933.1 96.3 %all-reduce.8.cloned.1.call-start = ((), (), s32[]{:S(2)}) async-start(), calls=%async_computation.2 | async-start | bytes 1835008 | tf_op jit(solution)/shard_map/while/body/eval_jaxpr/psum | solution.py:11
  1034.6 95.0 %all-reduce.8.cloned.1.call-start = ((), (), s32[]{:S(2)}) async-start(), calls=%async_computation.2 | async-start | bytes 1835008 | tf_op jit(solution)/shard_map/while/body/eval_jaxpr/psum | solution.py:11
  1134.8 94.8 %all-reduce.8.cloned.1.call-start = ((), (), s32[]{:S(2)}) async-start(), calls=%async_computation.2 | async-start | bytes 1835008 | tf_op jit(solution)/shard_map/while/body/eval_jaxpr/psum | solution.py:11
  1234.8 96.0 %all-reduce.8.cloned.1.call-start = ((), (), s32[]{:S(2)}) async-start(), calls=%async_computation.2 | async-start | bytes 1835008 | tf_op jit(solution)/shard_map/while/body/eval_jaxpr/psum | solution.py:11
  1336.1 95.8 %all-reduce.8.cloned.1.call-start = ((), (), s32[]{:S(2)}) async-start(), calls=%async_computation.2 | async-start | bytes 1835008 | tf_op jit(solution)/shard_map/while/body/eval_jaxpr/psum | solution.py:11
  1437.1 95.7 %all-reduce.8.cloned.1.call-start = ((), (), s32[]{:S(2)}) async-start(), calls=%async_computation.2 | async-start | bytes 1835008 | tf_op jit(solution)/shard_map/while/body/eval_jaxpr/psum | solution.py:11
  1538.0 96.1 %all-reduce.8.cloned.1.call-start = ((), (), s32[]{:S(2)}) async-start(), calls=%async_computation.2 | async-start | bytes 1835008 | tf_op jit(solution)/shard_map/while/body/eval_jaxpr/psum | solution.py:11
  1639.4 97.5 %all-reduce.8.cloned.1.call-start = ((), (), s32[]{:S(2)}) async-start(), calls=%async_computation.2 | async-start | bytes 1835008 | tf_op jit(solution)/shard_map/while/body/eval_jaxpr/psum | solution.py:11
  1742.1 97.5 %all-reduce.8.cloned.1.call-start = ((), (), s32[]{:S(2)}) async-start(), calls=%async_computation.2 | async-start | bytes 1835008 | tf_op jit(solution)/shard_map/while/body/eval_jaxpr/psum | solution.py:11
  1844.9 96.3 %all-reduce.8.cloned.1.call-start = ((), (), s32[]{:S(2)}) async-start(), calls=%async_computation.2 | async-start | bytes 1835008 | tf_op jit(solution)/shard_map/while/body/eval_jaxpr/psum | solution.py:11
  1946.4 96.0 %all-reduce.8.cloned.1.call-start = ((), (), s32[]{:S(2)}) async-start(), calls=%async_computation.2 | async-start | bytes 1835008 | tf_op jit(solution)/shard_map/while/body/eval_jaxpr/psum | solution.py:11
  2047.6 97.1 %all-reduce.8.cloned.1.call-start = ((), (), s32[]{:S(2)}) async-start(), calls=%async_computation.2 | async-start | bytes 1835008 | tf_op jit(solution)/shard_map/while/body/eval_jaxpr/psum | solution.py:11
  2150.0 96.7 %all-reduce.8.cloned.1.call-start = ((), (), s32[]{:S(2)}) async-start(), calls=%async_computation.2 | async-start | bytes 1835008 | tf_op jit(solution)/shard_map/while/body/eval_jaxpr/psum | solution.py:11
  2251.9 65.7 %all-reduce.6.cloned.1.call-start = ((), (), s32[]{:S(2)}) async-start(), calls=%async_computation.1 | async-start | bytes 2621440 | tf_op jit(solution)/shard_map/psum | solution.py:11
  2254.2 16.7 dynamic-slice-start
  2317.7 13.0 copy-start.4
  2317.7 13.1 copy-start.2
Sparse Core Ops, SparseCore 0:
  10.3 35.6 all-gather.2
  647.0 79.4 all-reduce.7
  736.4 90.2 all-reduce.7
  836.4 91.4 all-reduce.7
  937.5 91.8 all-reduce.7
  1039.0 90.6 all-reduce.7
  1139.5 90.0 all-reduce.7
  1239.5 91.2 all-reduce.7
  1340.7 91.1 all-reduce.7
  1441.5 91.2 all-reduce.7
  1542.7 91.4 all-reduce.7
  1643.8 93.0 all-reduce.7
  1746.8 92.7 all-reduce.7
  1849.2 91.8 all-reduce.7
  1950.7 91.5 all-reduce.7
  2051.9 92.7 all-reduce.7
  2154.3 92.3 all-reduce.7
  2255.5 62.1 all-reduce.5
where the time goes:
time: 2360 us; the launch traced here: 2340 us
  waiting for transfers between devices  1570 us (67%)
  other arithmetic  420 us (18%)
  matrix products  200 us (8%)
  local copies, waits for them, and re-layouts  116 us (5%)
  between operations  24.5 us (1%)
    psum x17, waiting for transfers between devices, from_root(): return lax.psum(jnp.where(mine, x, jnp.zeros_like(x)), axis)  1550 us
    another operation x62, other arithmetic, local(): factor = jnp.linalg.cholesky(diag_block)  356 us
    another operation x30, matrix products, local(): factor = jnp.linalg.cholesky(diag_block)  92.4 us
    dot_general x16, matrix products, chain_step(): jnp.dot(finished, coupling.T, precision=lax.Precision.HIGHEST, preferred_...  48.5 us
  transfers between devices with their start and end apart: 18, of which 18 were waited for; matrix products, arithmetic and copies ran while one was open for 1% of the time, Pallas kernels for 0%

commit v1 on v0

v1 whole, which is shorter than its diff:
```python
import functools

import jax
import jax.numpy as jnp
from jax import lax
from jax.experimental import pallas as pl
from jax.experimental.pallas import tpu as pltpu
from jax.sharding import PartitionSpec as P

PANEL = 2048
F32 = jnp.float32
BF16 = jnp.bfloat16
NN = (((1,), (0,)), ((), ()))
NT = (((1,), (1,)), ((), ()))
TN = (((0,), (0,)), ((), ()))
MICRO = 32
TILE = 256


def split(x):
    high = x.astype(BF16)
    return high, (x - high.astype(F32)).astype(BF16)


def product(left, right, dims):
    (lc,), (rc,) = dims[0]
    lh, ll = left
    rh, rl = right
    return lax.dot_general(
        jnp.concatenate([lh, ll, lh], lc),
        jnp.concatenate([rh, rh, rl], rc),
        dims,
        preferred_element_type=F32,
    )


def lanes(v, q):
    return jnp.broadcast_to(v[:, q : q + 1], (8, 128))


def sublanes(v, s):
    return jnp.broadcast_to(v[s : s + 1, :], (8, 128))


def micro_rows(work, base, size):
    groups = size // 8
    left = [work[base + 8 * i : base + 8 * i + 8, 0:128] for i in range(groups)]
    right = [work[base + 8 * i : base + 8 * i + 8, 128:256] for i in range(groups)]
    cols = [[lanes(left[i], base + q) for q in range(8 * i + 8)] for i in range(groups)]
    sub = lax.broadcasted_iota(jnp.int32, (8, 128), 0)
    for k in range(size):
        ik, sk = k // 8, k % 8
        inverse = 1.0 / sublanes(cols[ik][k], sk)
        row_left, row_right = sublanes(left[ik], sk), sublanes(right[ik], sk)
        scaled = {q: sublanes(cols[q // 8][k], q % 8) * inverse for q in range(k + 1, size)}
        for i in range(ik, groups):
            raw = cols[i][k]
            if i == ik:
                if sk == 7:
                    continue
                raw = jnp.where(sub > sk, raw, 0.0)
            factor = raw * inverse
            left[i] = left[i] - factor * row_left
            right[i] = right[i] - factor * row_right
            for q in range(k + 1, 8 * i + 8):
                cols[i][q] = cols[i][q] - raw * scaled[q]
    out = []
    for i in range(groups):
        pivots = cols[i][8 * i]
        for s in range(1, 8):
            pivots = jnp.where(sub == s, cols[i][8 * i + s], pivots)
        scale = lax.rsqrt(pivots)
        out.append(jnp.concatenate([left[i] * scale, right[i] * scale], 1))
    return jnp.concatenate(out, 0)


def factor_128(work, block):
    r = lax.broadcasted_iota(jnp.int32, (128, 128), 0)
    c = lax.broadcasted_iota(jnp.int32, (128, 128), 1)
    work[:, 0:128] = block
    work[:, 128:256] = jnp.where(r == c, 1.0, 0.0)
    for base in range(0, 128, MICRO):
        rows = micro_rows(work, base, MICRO)
        work[base : base + MICRO, :] = rows
        if base + MICRO < 128:
            high, low = split(rows)
            update = product((high[:, :128], low[:, :128]), (high, low), TN)
            work[base + MICRO :, :] = work[base + MICRO :, :] - update[base + MICRO :, :]
    lower = jnp.where(r >= c, work[:, 0:128].T, 0.0)
    inverse = jnp.where(r >= c, work[:, 128:256], 0.0)
    return lower, inverse


def factor_kernel(pos, a_in, top_ref, y_ref, a, inv, parts, work, rhs, sem):
    copy = pltpu.make_async_copy(a_in, a, sem)
    copy.start()
    copy.wait()
    tiles = PANEL // TILE
    row_id, col_id = pos[0], pos[1]

    def at(i):
        return pl.ds(pl.multiple_of(i * TILE, TILE), TILE)

    def outer(j, carry):
        o = j * TILE
        here = at(j)
        first = pl.ds(pl.multiple_of(o, 128), 128)
        second = pl.ds(pl.multiple_of(o + 128, 128), 128)
        l11, x11 = factor_128(work, a[first, first])
        x11s = split(x11)
        l21 = product(split(a[second, first]), x11s, NT)
        l21s = split(l21)
        d22 = a[second, second] - product(l21s, l21s, NT)
        l22, x22 = factor_128(work, d22)
        x21 = -product(split(x22), split(product(l21s, x11s, NN)), NN)
        zero = jnp.zeros((128, 128), F32)
        a[first, here] = jnp.concatenate([l11, zero], 1)
        a[second, here] = jnp.concatenate([l21, l22], 1)
        xj = jnp.concatenate([jnp.concatenate([x11, zero], 1), jnp.concatenate([x21, x22], 1)], 0)
        inv[j] = xj
        xjs = split(xj)

        def panel(i, carry):
            p = product(split(a[at(i), here]), xjs, NT)
            a[at(i), here] = p
            high, low = split(p)
            parts[at(i), 0:TILE] = high
            parts[at(i), TILE : 2 * TILE] = low
            return carry

        lax.fori_loop(j + 1, tiles, panel, 0)
        extra = pl.ds(PANEL, 128)
        p = product(split(a[extra, here]), xjs, NT)
        a[extra, here] = p
        ps = split(p)

        def columns(t, carry):
            right = (parts[at(t), 0:TILE], parts[at(t), TILE : 2 * TILE])

            def rows(i, carry):
                left = (parts[at(i), 0:TILE], parts[at(i), TILE : 2 * TILE])
                a[at(i), at(t)] = a[at(i), at(t)] - product(left, right, NT)
                return carry

            lax.fori_loop(t, tiles, rows, 0)
            a[extra, at(t)] = a[extra, at(t)] - product(ps, right, NT)
            return carry

        lax.fori_loop(j + 1, tiles, columns, 0)
        return carry

    lax.fori_loop(0, tiles, outer, 0)
    r = lax.broadcasted_iota(jnp.int32, (128, PANEL), 0)
    c = lax.broadcasted_iota(jnp.int32, (128, PANEL), 1)
    rhs[0:128, :] = jnp.where(c == r + col_id * 128, 1.0, 0.0)
    rhs[128:256, :] = a[PANEL : PANEL + 128, :]

    def back(step, carry):
        j = tiles - 1 - step
        here = at(j)
        y = product(split(rhs[:, here]), split(inv[j]), NN)
        y_ref[:, here] = y
        ys = split(y)

        def earlier(back_by, carry):
            t = j - 1 - back_by
            rhs[:, at(t)] = rhs[:, at(t)] - product(ys, split(a[here, at(t)]), NN)
            return carry

        lax.fori_loop(0, j, earlier, 0)
        return carry

    lax.fori_loop(0, tiles, back, 0)
    rr = pl.ds(pl.multiple_of(row_id * TILE, TILE), TILE)
    cc = pl.ds(pl.multiple_of(col_id * 128, 128), 128)
    gr = lax.broadcasted_iota(jnp.int32, (TILE, 128), 0) + row_id * TILE
    gc = lax.broadcasted_iota(jnp.int32, (TILE, 128), 1) + col_id * 128
    top_ref[...] = jnp.where(gr >= gc, a[rr, cc], 0.0)


def factor_panel(position, system):
    return pl.pallas_call(
        factor_kernel,
        out_shape=[jax.ShapeDtypeStruct((TILE, 128), F32), jax.ShapeDtypeStruct((256, PANEL), F32)],
        in_specs=[pl.BlockSpec(memory_space=pltpu.SMEM), pl.BlockSpec(memory_space=pl.ANY)],
        out_specs=[pl.BlockSpec(memory_space=pltpu.VMEM)] * 2,
        scratch_shapes=[
            pltpu.VMEM((PANEL + 128, PANEL), F32),
            pltpu.VMEM((PANEL // TILE, TILE, TILE), F32),
            pltpu.VMEM((PANEL, 2 * TILE), BF16),
            pltpu.VMEM((128, 256), F32),
            pltpu.VMEM((256, PANEL), F32),
            pltpu.SemaphoreType.DMA,
        ],
        name="factor_panel",
    )(position, system)


def kernel_block(left_rows, right_rows):
    products = jnp.dot(
        left_rows, right_rows.T, precision=lax.Precision.HIGH, preferred_element_type=jnp.float32
    )
    left_square = jnp.sum(left_rows * left_rows, axis=1)
    right_square = jnp.sum(right_rows * right_rows, axis=1)
    distance = left_square[:, None] + right_square[None, :] - 2.0 * products
    return jnp.exp(-distance / left_rows.shape[1])


def local(features, jitter):
    n_rowdev = lax.axis_size("row")
    n_coldev = lax.axis_size("col")
    local_rows, feat = features.shape
    band_rows = PANEL // n_rowdev
    slab_cols = PANEL // n_coldev
    below_count = local_rows - band_rows
    row_id = lax.axis_index("row")
    col_id = lax.axis_index("col")
    own_jitter = jnp.pad(jitter[:band_rows][None, :], ((0, 7), (0, feat - band_rows)))
    gathered = lax.all_gather(jnp.concatenate([features[:band_rows], own_jitter], 0), "row", axis=0)
    panel_feats = gathered[:, :band_rows].reshape(PANEL, feat)
    panel_jitter = gathered[:, band_rows, :band_rows].reshape(PANEL)
    share = band_rows // slab_cols
    sends = []
    for c in range(n_coldev):
        for r in range(n_rowdev):
            source_col = (c % share) * n_rowdev + r
            sends.append(((c // share) * n_coldev + source_col, r * n_coldev + c))
    ahead_piece = lax.dynamic_slice_in_dim(
        features, band_rows + (col_id // n_rowdev) * slab_cols, slab_cols, 0
    )
    ahead_feats = lax.ppermute(ahead_piece, ("row", "col"), sends)
    system = kernel_block(jnp.concatenate([panel_feats, ahead_feats], 0), panel_feats)
    r = lax.broadcasted_iota(jnp.int32, system.shape, 0)
    c = lax.broadcasted_iota(jnp.int32, system.shape, 1)
    system = jnp.where(r == c, 1.0 + panel_jitter[None, :], system)
    position = jnp.stack([row_id, col_id]).astype(jnp.int32)
    top_rows, solve = factor_panel(position, system)

    below_feats = features[band_rows:]
    below = kernel_block(below_feats, panel_feats)
    ahead_tile = kernel_block(below_feats, ahead_feats)
    row_pos = lax.broadcasted_iota(jnp.int32, (below_count, slab_cols), 0)
    col_pos = lax.broadcasted_iota(jnp.int32, (below_count, slab_cols), 1)
    match_mask = (row_pos < band_rows) & (
        row_id * band_rows + row_pos == col_id * slab_cols + col_pos
    )
    ahead_tile = jnp.where(match_mask, 1.0 + jitter[band_rows:][:, None], ahead_tile)
    both = jnp.dot(below, solve.T, precision=lax.Precision.HIGH, preferred_element_type=jnp.float32)
    lower_out = jnp.concatenate([top_rows, both[:, :slab_cols]], axis=0)
    ahead_out = jnp.concatenate(
        [jnp.zeros((band_rows, slab_cols), jnp.float32), ahead_tile - both[:, slab_cols:]], axis=0
    )
    return (lower_out, ahead_out)


def solution(mesh):
    return jax.shard_map(
        local,
        mesh=mesh,
        in_specs=(P("row", None), P("row")),
        out_specs=(P("row", "col"), P("row", "col")),
        check_vma=False,
    )
```

time: 2360 us -> 235 us (0.10)
  waiting for transfers between devices: 1570 us -> 31.8 us
  other arithmetic: 420 us -> 9.8 us
  matrix products: 200 us -> 49.2 us
  Pallas kernels: 0 us -> 120 us
  local copies, waits for them, and re-layouts: 116 us -> 3.86 us
    psum x17 -> x0, waiting for transfers between devices: 1550 us -> none  [from_root(): return lax.psum(jnp.where(mine, x, jnp.zeros_like(x)), axis)]
    another operation x64 -> x1, other arithmetic: 365 us -> 0.61 us  [local(): position = jnp.stack([row_id, col_id]).astype(jnp.int32)]
    pallas_call x0 -> x1, Pallas kernels: none -> 120 us  [factor_panel(): pl.pallas_call(factor_kernel, out_shape=[jax.ShapeDtypeStruct((TILE, 128)...]
    another operation x31 -> x0, matrix products: 93.4 us -> none  [the longest x30 92.4 us: local(): factor = jnp.linalg.cholesky(diag_block)]
    dot_general x20 -> x4, matrix products: 106 us -> 49.2 us  [the longest x3 37 us: kernel_block(): jnp.dot(left_rows, right_rows.T, precision=lax.Precision.HIGH, preferred_...]
    dynamic_update_slice x16 -> x0, local copies, waits for them, and re-layouts: 35.1 us -> none  [chain_step(): lax.dynamic_update_slice_in_dim(collected, finished, source * slab_cols, 1)]
    select_n x19 -> x0, other arithmetic: 27.3 us -> none  [the longest x18 19.7 us: from_root(): return lax.psum(jnp.where(mine, x, jnp.zeros_like(x)), axis)]
  transfers between devices with their start and end apart: 18 -> 2, of which waited for: 18 -> 1; matrix products, arithmetic and copies ran while one was open for 1% -> 2% of each run, Pallas kernels for 0% -> 0%
where the time goes in v1:
time: 235 us
  Pallas kernels  120 us (51%)
  matrix products  49.2 us (21%)
  waiting for transfers between devices  31.8 us (14%)
  between operations  14.2 us (6%)
  other arithmetic  9.8 us (4%)
  starting transfers between devices  6.07 us (3%)
  local copies, waits for them, and re-layouts  3.86 us (2%)
    pallas_call x1, Pallas kernels, factor_panel(): pl.pallas_call(factor_kernel, out_shape=[jax.ShapeDtypeStruct((TILE, 128)...  120 us
    dot_general x3, matrix products, kernel_block(): jnp.dot(left_rows, right_rows.T, precision=lax.Precision.HIGH, preferred_...  37 us
    all_gather x1, waiting for transfers between devices, local(): lax.all_gather(jnp.concatenate([features[:band_rows], own_jitter], 0), 'r...  31.7 us
    dot_general x1, matrix products, local(): jnp.dot(below, solve.T, precision=lax.Precision.HIGH, preferred_element_t...  12.1 us
    ppermute x1, starting transfers between devices, local(): ahead_feats = lax.ppermute(ahead_piece, ('row', 'col'), sends)  6.03 us
  transfers between devices with their start and end apart: 2, of which 1 were waited for; matrix products, arithmetic and copies ran while one was open for 2% of the time, Pallas kernels for 0%

profile of v1, /device:TPU:1, one launch (start us, length us, event | category | flops | bytes accessed | tf_op | source)
XLA Modules:
  0.0 234.8 jit_solution(17749926419040401837)
XLA Ops:
  7.2 0.0 all-gather.3.cloned.1.call-start
  7.2 1.1 slice.24
  8.3 0.7 slice.25
  9.0 0.8 select_maximum_fusion
  9.8 0.0 all-gather.3.cloned.1.call-update
  9.9 1.0 constant_dynamic-slice_fusion
  10.8 6.0 %collective-permute-start = (f32[128,512]{1,0:T(8,128)S(1)}, f32[128,512]{1,0:T(8,128)S(1)}, u32[]{:S(2)}, u32[]{:S(2)}) collective-permute-start(f32[128,512]{1,0:T(8,128)S(1)} %constant_dynamic-slice_fusion), channel_id=1, source_target_pairs={{0,0},{1,16},{2,32},{3,48},{4,64},{5,80},{6,96},{7,112},{8,1},{9,1... | collective-permute-start | bytes 786440 | tf_op jit(solution)/shard_map/ppermute | solution.py:231
  16.9 0.6 pad_add_fusion.pos
  17.5 0.7 slice_add_fusion.1
  18.2 2.4 %multiply_reduce_fusion.1 = f32[1792]{0:T(1024)S(1)} fusion(f32[2048,512]{1,0:T(8,128)} %param.2), kind=kLoop, calls=%fused_computation.17 | loop fusion | flops 1833216 | bytes 3677184 | tf_op jit(solution)/shard_map/reduce_sum | solution.py:203
  20.6 0.0 collective-permute-done
  20.6 0.1 multiply_reduce_fusion.2
  20.7 31.7 %all-gather.3.cloned.1.call-done = f32[2112,512]{1,0:T(8,128)} async-done(((f32[264,512]{1,0:T(8,128)}), f32[2112,512]{1,0:T(8,128)}) %all-gather.3.cloned.1.call-update) | async-done | bytes 4325392 | tf_op jit(solution)/shard_map/all_gather | solution.py:219
  52.4 0.0 copy-start
  52.5 2.9 %multiply_reduce_fusion = (f32[8,256]{1,0:T(8,128)S(1)}, f32[8,256,512]{2,1,0:T(8,128)S(1)}) fusion(f32[8,264,512]{2,1,0:T(8,128)} %bitcast.28), kind=kLoop, calls=%fused_computation.16 | loop fusion | flops 2095104 | bytes 8396800 | tf_op jit(solution)/shard_map/reduce_sum | solution.py:204
  55.4 0.8 slice_add_fusion
  56.2 0.0 copy-done
  56.2 14.7 %fusion.15 = f32[2048,1792]{0,1:T(8,128)} fusion(f32[2048,512]{1,0:T(8,128)S(1)} %bitcast.25, f32[2048,512]{1,0:T(8,128)S(1)} %copy-done), kind=kOutput, calls=%fused_computation.20 | convolution fusion | flops 11274289152 | bytes 22544384 | tf_op jit(solution)/shard_map/dot_general | solution.py:200
  70.9 0.4 fusion.12
  71.3 20.5 %exponential_select_fusion.a_in = f32[2176,2048]{1,0:T(8,128)} fusion(f32[2048,512]{1,0:T(8,128)S(1)} %bitcast.27, f32[2048]{0:T(1024)S(1)} %bitcast.31, f32[2176]{0:T(1024)S(1)} %fusion.12, f32[2048]{0:T(1024)S(1)} %bitcast.33, f32[128,512]{1,0:T(8,128)S(1)} %collective-permute-done), kind=kOutput, calls=%fused_computation | convolution fusion | flops 13722517504 | bytes 22307328 | tf_op jit(solution)/shard_map/dot_general | solution.py:200
  91.8 120.0 %factor_panel.1 = (f32[256,128]{1,0:T(8,128)}, f32[256,2048]{1,0:T(8,128)}) custom-call(s32[2]{0:T(128)} %pad_add_fusion.pos, f32[2176,2048]{1,0:T(8,128)} %exponential_select_fusion.a_in), custom_call_target="tpu_custom_call" | custom-call | tf_op jit(solution)/shard_map/factor_panel/pallas_call | solution.py:182
  211.8 0.0 copy-start.1
  211.8 12.1 %fusion.3 = f32[1792,256]{1,0:T(8,128)S(1)} fusion(f32[256,2048]{1,0:T(8,128)} %get-tuple-element.5, f32[2048,1792]{0,1:T(8,128)} %fusion.15, f32[2048]{0:T(1024)S(1)} %bitcast.32, f32[1792]{0:T(1024)S(1)} %multiply_reduce_fusion.1), kind=kOutput, calls=%fused_computation.6 | convolution fusion | flops 5655494656 | bytes 18627584 | tf_op jit(solution)/shard_map/dot_general | solution.py:248
  224.0 0.0 copy-start.2
  224.0 0.1 slice.34
  224.0 0.0 copy-done.1
  224.1 1.8 slice_subtract_fusion
  225.9 1.0 concatenate.15
  226.9 0.0 copy-done.2
  226.9 1.0 pad_maximum_fusion.2
  (4 shorter events, 0.0 us)
Async XLA Ops:
  7.2 45.3 %all-gather.3.cloned.1.call-start = ((), (), s32[]{:S(2)}) async-start(), calls=%async_computation | async-start | bytes 4866048 | tf_op jit(solution)/shard_map/all_gather | solution.py:219
  10.8 9.7 %collective-permute-start = (f32[128,512]{1,0:T(8,128)S(1)}, f32[128,512]{1,0:T(8,128)S(1)}, u32[]{:S(2)}, u32[]{:S(2)}) collective-permute-start(f32[128,512]{1,0:T(8,128)S(1)} %constant_dynamic-slice_fusion), channel_id=1, source_target_pairs={{0,0},{1,16},{2,32},{3,48},{4,64},{5,80},{6,96},{7,112},{8,1},{9,1... | collective-permute-start | bytes 786440 | tf_op jit(solution)/shard_map/ppermute | solution.py:231
  52.4 3.8 %copy-start = (f32[2048,512]{1,0:T(8,128)S(1)}, f32[2048,512]{1,0:T(8,128)}, u32[]{:S(2)}) copy-start(f32[2048,512]{1,0:T(8,128)} %param.2) | copy-start | bytes 12582916
  211.8 12.2 %copy-start.1 = (f32[2048,512]{1,0:T(8,128)S(1)}, f32[2048,512]{1,0:T(8,128)}, u32[]{:S(2)}) copy-start(f32[2048,512]{1,0:T(8,128)} %param.2) | copy-start | bytes 12582916
  224.0 3.0 %copy-start.2 = (f32[256,128]{1,0:T(8,128)S(1)}, f32[256,128]{1,0:T(8,128)}, u32[]{:S(2)}) copy-start(f32[256,128]{1,0:T(8,128)} %get-tuple-element.4) | copy-start | bytes 393220
Sparse Core Ops, SparseCore 0:
  10.2 42.1 all-gather.2
